TPU v7x, 32 devices: a whole 2x2x4 slice. The times are simulated.
32 devices in a mesh: frames: 8 (over z, x), heads: 4 (over y, core).
Axes of the slice: x: 2, y: 2, z: 4, core: 2. Of those that a mesh axis runs over, the one named last changes fastest.
Arguments:
- queries: bfloat16 [1024, 4096], P('frames', 'heads'), may hold values from -9 to 9
- keys: bfloat16 [1024, 512], P(('frames', 'heads')), may hold values from -4.5 to 4.5
- values: bfloat16 [1024, 512], P(('frames', 'heads')), may hold values from -6 to 6
- block_mask: int32 [8, 8], replicated, may hold values from 0 to 1, as said below
- lengths: int32 [8], replicated, may hold values from 64 to 128, as said below
Outputs:
- attended: bfloat16 [1024, 4096], P('frames', 'heads')
Inputs may be any that keep to these rules, and one draw needn't show every extreme that they name: block_mask[i, i] = 1 and block_mask[i, j] = 0 for j > i. `lengths`: some frame group is full in every draw.
All inputs are finite; a program needn't handle non-finite values.
Results may differ from a plain program's by a relative error of at most 0.0055.
Values may be sent and summed in bfloat16 or wider, within the bound.
A program may use at most 64 MiB of HBM per device.

v0:
```python
import math

import jax
import jax.numpy as jnp
from jax import lax
from jax.sharding import PartitionSpec as P

HEAD_DIM = 128


masked_score = -1e30


def attend(query_sets, keys_mine, values_mine, block_mask, lengths, group_tokens):
    kv_local = keys_mine.shape[1] // HEAD_DIM
    q_local = query_sets[0][0].shape[1] // HEAD_DIM
    per_kv = q_local // kv_local
    scale = HEAD_DIM ** (-0.5)
    group_count = block_mask.shape[0]
    group_ids = jnp.arange(group_count, dtype=jnp.int32)
    prepared = []
    initial = []
    for rows, owner in query_sets:
        count = rows.shape[0]
        prepared.append(
            (
                rows.reshape(count, kv_local, per_kv, HEAD_DIM),
                lax.dynamic_slice_in_dim(block_mask, owner, 1, 0)[0],
            )
        )
        initial.append(
            (
                jnp.full((kv_local, per_kv, count), masked_score, jnp.float32),
                jnp.zeros((kv_local, per_kv, count), jnp.float32),
                jnp.zeros((count, kv_local, per_kv, HEAD_DIM), jnp.float32),
            )
        )
    key_piece = lax.all_gather(keys_mine, "frames", axis=0, tiled=True)
    value_piece = lax.all_gather(values_mine, "frames", axis=0, tiled=True)
    fold_rows = key_piece.shape[0]
    width = math.gcd(fold_rows, 512)
    blocks = fold_rows // width
    key_blocks = key_piece.reshape(blocks, width, kv_local, HEAD_DIM)
    value_blocks = value_piece.reshape(blocks, width, kv_local, HEAD_DIM)

    def one_block(state, inputs):
        key_block, value_block, number = inputs
        positions = number * width + jnp.arange(width, dtype=jnp.int32)
        key_group = positions // group_tokens
        within = positions % group_tokens
        onehot = (key_group[:, None] == group_ids[None, :]).astype(jnp.int32)
        live_len = jnp.sum(onehot * lengths[None, :], axis=1)
        updated = []
        for (query_rows, mask_row), (running_max, running_total, running_acc) in zip(
            prepared, state
        ):
            allowed = jnp.sum(onehot * mask_row[None, :], axis=1)
            valid = (allowed > 0) & (within < live_len)

            def update(current):
                old_max, old_total, old_acc = current
                scores = (
                    jnp.einsum(
                        "tkgd,skd->kgts", query_rows, key_block, preferred_element_type=jnp.float32
                    )
                    * scale
                )
                scores = jnp.where(valid[None, None, None, :], scores, masked_score)
                new_max = jnp.maximum(old_max, jnp.max(scores, axis=-1))
                probs = jnp.exp(scores - new_max[..., None])
                factor = jnp.exp(old_max - new_max)
                new_total = old_total * factor + jnp.sum(probs, axis=-1)
                added = jnp.einsum(
                    "kgts,skd->tkgd",
                    probs.astype(jnp.bfloat16),
                    value_block,
                    preferred_element_type=jnp.float32,
                )
                new_acc = old_acc * jnp.transpose(factor, (2, 0, 1))[..., None] + added
                return (new_max, new_total, new_acc)

            updated.append(
                lax.cond(
                    jnp.any(valid),
                    update,
                    lambda current: current,
                    (running_max, running_total, running_acc),
                )
            )
        return (tuple(updated), None)

    numbers = jnp.arange(blocks, dtype=jnp.int32)
    final, unused = lax.scan(one_block, tuple(initial), (key_blocks, value_blocks, numbers))
    results = []
    for (rows, owner), (running_max, running_total, running_acc) in zip(query_sets, final):
        output = running_acc / jnp.transpose(running_total, (2, 0, 1))[..., None]
        results.append(output.astype(jnp.bfloat16).reshape(rows.shape[0], q_local * HEAD_DIM))
    return results


def local(queries, keys, values, block_mask, lengths):
    keys_mine, values_mine = (
        lax.all_to_all(keys, "heads", split_axis=1, concat_axis=0, tiled=True),
        lax.all_to_all(values, "heads", split_axis=1, concat_axis=0, tiled=True),
    )
    group_tokens = queries.shape[0]
    frame_index = lax.axis_index("frames")
    outputs = attend(
        [(queries, frame_index)], keys_mine, values_mine, block_mask, lengths, group_tokens
    )
    return outputs[0]


def solution(mesh):
    return jax.shard_map(
        local,
        mesh=mesh,
        in_specs=(
            P("frames", "heads"),
            P(("frames", "heads"), None),
            P(("frames", "heads"), None),
            P(),
            P(),
        ),
        out_specs=P("frames", "heads"),
        check_vma=False,
    )
```

profile of v0, /device:TPU:30, one launch (start us, length us, event | category | flops | bytes accessed | tf_op | source)
XLA Modules:
  0.0 84.3 jit_solution(984634713009666700)
XLA Ops:
  0.0 0.0 copy-start
  0.0 0.8 copy-done
  0.8 0.0 copy-start.1
  0.8 0.6 copy_bitcast_fusion
  1.4 3.7 %all-to-all-start.1 = ((bf16[32,4,128]{2,0,1:T(8,128)(2,1)}), bf16[32,4,128]{2,0,1:T(8,128)(2,1)S(1)}, u32[]{:S(2)}, u32[]{:S(2)}) async-start(bf16[32,4,128]{2,0,1:T(8,128)(2,1)} %copy_bitcast_fusion), calls=%async_computation.1 | async-start | bytes 65536 | tf_op jit(solution)/shard_map/all_to_all | solution.py:104
  5.1 1.4 %copy_bitcast_fusion.1 = bf16[32,4,128]{2,0,1:T(8,128)(2,1)} fusion(bf16[32,512]{1,0:T(8,128)(2,1)} %param.10), kind=kLoop, calls=%fused_computation.47 | loop fusion | bytes 65536 | tf_op jit(solution)/shard_map/all_to_all | solution.py:103
  6.5 0.7 constant_dynamic-slice_fusion
  7.2 1.1 %copy.37 = bf16[128,1024]{0,1:T(8,128)(2,1)S(1)} copy(bf16[128,1024]{1,0:T(8,128)(2,1)} %param.9) | data formatting | bytes 524288 | tf_op args[0]
  8.3 0.2 copy.39
  8.5 0.0 all-to-all-done.1
  8.5 3.8 %all-to-all-start = ((bf16[32,4,128]{2,0,1:T(8,128)(2,1)}), bf16[32,4,128]{2,0,1:T(8,128)(2,1)S(1)}, u32[]{:S(2)}, u32[]{:S(2)}) async-start(bf16[32,4,128]{2,0,1:T(8,128)(2,1)} %copy_bitcast_fusion.1), calls=%async_computation | async-start | bytes 65536 | tf_op jit(solution)/shard_map/all_to_all | solution.py:103
  12.3 30.8 %all_gather.7 = bf16[1024,128]{1,0:T(8,128)(2,1)S(1)} all-gather(bf16[128,128]{1,0:T(8,128)(2,1)S(1)} %bitcast.97), channel_id=1, replica_groups=mesh['frames'=8,'heads'=4] {'frames'}, dimensions={0}, use_global_device_ids=true | all-gather | bytes 294912 | tf_op jit(solution)/shard_map/all_gather | solution.py:39
  43.1 0.1 copy.40
  43.3 0.0 all-to-all-done
  43.3 30.7 %all_gather.6 = bf16[1024,128]{1,0:T(8,128)(2,1)S(1)} all-gather(bf16[128,128]{1,0:T(8,128)(2,1)S(1)} %bitcast.98), channel_id=1, replica_groups=mesh['frames'=8,'heads'=4] {'frames'}, dimensions={0}, use_global_device_ids=true | all-gather | bytes 294912 | tf_op jit(solution)/shard_map/all_gather | solution.py:38
  74.1 0.0 copy-done.1
  74.1 9.3 %while.17 = (s32[]{:T(128)}, f32[1,8,128]{2,1,0:T(8,128)S(1)}, f32[1,8,128]{2,1,0:T(8,128)S(1)}, f32[128,1,8,128]{0,3,2,1:T(8,128)S(1)}, s32[2]{0:T(128)S(1)}, /...) while((s32[]{:T(128)}, f32[1,8,128]{2,1,0:T(8,128)S(1)}, ...), condition=%wide.region_8.9_spmd.clone, body=%wide.region_0.8_spmd.clone.sunk | while | flops 274503680 | bytes 7944539 | solution.py:93
  74.1 0.6 dynamic_slice.43
  75.3 0.1 fusion.38
  75.4 0.7 fusion.39
  76.9 1.9 %conditional.3 = ((f32[1,8,128]{2,1,0:T(8,128)S(1)}, f32[1,8,128]{2,1,0:T(8,128)S(1)}, f32[128,1,8,128]{0,3,2,1:T(8,128)S(1)})) conditional(s32[]{:T(128)} %convert_element_type.23, (f32[1,8,128]{2,1,0:T(8,128)S(1)}, f32[1,8,128]{2,1,0:T(8,128)S(1)}, f32[128,1,8,128]{0,3,2,1:T(8,128)S(1)}) %tuple.59, (pred[512]{0:T(512)(128)(4,1)S(1)}, ...), branch_computations={%region_4.4_spmd, %region_5.7_spmd} | conditional | flops 274467840 | bytes 7931432 | solution.py:83
  76.9 0.5 bitcast_reduce_fusion
  77.4 0.8 fusion.5
  78.2 0.5 fusion.4
  78.7 0.6 dynamic_slice.43
  80.0 0.1 fusion.38
  80.1 0.7 fusion.39
  81.5 1.9 %conditional.3 = ((f32[1,8,128]{2,1,0:T(8,128)S(1)}, f32[1,8,128]{2,1,0:T(8,128)S(1)}, f32[128,1,8,128]{0,3,2,1:T(8,128)S(1)})) conditional(s32[]{:T(128)} %convert_element_type.23, (f32[1,8,128]{2,1,0:T(8,128)S(1)}, f32[1,8,128]{2,1,0:T(8,128)S(1)}, f32[128,1,8,128]{0,3,2,1:T(8,128)S(1)}) %tuple.59, (pred[512]{0:T(512)(128)(4,1)S(1)}, ...), branch_computations={%region_4.4_spmd, %region_5.7_spmd} | conditional | flops 274467840 | bytes 7931432 | solution.py:83
  81.5 0.5 bitcast_reduce_fusion
  82.0 0.8 fusion.5
  82.9 0.5 fusion.4
  83.4 0.1 divide_convert_fusion
  83.5 0.9 %copy.43 = bf16[128,1024]{1,0:T(8,128)(2,1)} copy(bf16[128,1024]{0,1:T(8,128)(2,1)S(1)} %bitcast.93) | data formatting | bytes 524288 | tf_op jit(solution)/shard_map/reshape | solution.py:97
  (12 shorter events, 0.1 us)
Async XLA Ops:
  0.0 0.8 copy-start
  0.8 73.3 %copy-start.1 = (s32[8]{0:T(128)S(1)}, s32[8]{0:T(128)}, u32[]{:S(2)}) copy-start(s32[8]{0:T(128)} %param.13) | copy-start | bytes 100
  1.4 7.1 %all-to-all-start.1 = ((bf16[32,4,128]{2,0,1:T(8,128)(2,1)}), bf16[32,4,128]{2,0,1:T(8,128)(2,1)S(1)}, u32[]{:S(2)}, u32[]{:S(2)}) async-start(bf16[32,4,128]{2,0,1:T(8,128)(2,1)} %copy_bitcast_fusion), calls=%async_computation.1 | async-start | bytes 65536 | tf_op jit(solution)/shard_map/all_to_all | solution.py:104
  8.5 34.8 %all-to-all-start = ((bf16[32,4,128]{2,0,1:T(8,128)(2,1)}), bf16[32,4,128]{2,0,1:T(8,128)(2,1)S(1)}, u32[]{:S(2)}, u32[]{:S(2)}) async-start(bf16[32,4,128]{2,0,1:T(8,128)(2,1)} %copy_bitcast_fusion.1), calls=%async_computation | async-start | bytes 65536 | tf_op jit(solution)/shard_map/all_to_all | solution.py:103
where the time goes:
time: 84.8 us; the launch traced here: 84.3 us
  blocking collectives  61.6 us (73%)
  starting transfers between devices  7.53 us (9%)
  local copies, waits for them, and re-layouts  6.95 us (8%)
  loops' own time  2.87 us (3%)
  other arithmetic  2.72 us (3%)
  matrix products  2.59 us (3%)
    all_gather x1, blocking collectives, attend(): value_piece = lax.all_gather(values_mine, 'frames', axis=0, tiled=True)  30.8 us
    all_gather x1, blocking collectives, attend(): key_piece = lax.all_gather(keys_mine, 'frames', axis=0, tiled=True)  30.7 us
    all_to_all x1, starting transfers between devices, local(): lax.all_to_all(keys, 'heads', split_axis=1, concat_axis=0, tiled=True)  3.79 us
    all_to_all x1, starting transfers between devices, local(): lax.all_to_all(values, 'heads', split_axis=1, concat_axis=0, tiled=True)  3.74 us
    another operation x1, loops' own time, attend(): lax.scan(one_block, tuple(initial), (key_blocks, value_blocks, numbers))  2.76 us
    unnamed x7, local copies, waits for them, and re-layouts  2.2 us
  transfers between devices with their start and end apart: 2, of which 0 were waited for; matrix products, arithmetic and copies ran while one was open for 4% of the time, Pallas kernels for 0%

commit v1 on v0

v1 whole, which is shorter than its diff:
```python
import functools
import math

import jax
import jax.numpy as jnp
from jax import lax
from jax.experimental import pallas as pl
from jax.experimental.pallas import tpu as pltpu
from jax.sharding import PartitionSpec as P

HEAD_DIM = 128
MESH = pl.DeviceIdType.MESH
masked_score = -1e30


def kernel(
    frames,
    heads,
    lanes,
    mask_ref,
    len_ref,
    q_ref,
    k_ref,
    v_ref,
    out_ref,
    kv,
    qt,
    top,
    total,
    acc,
    send_sem,
    recv_sem,
    pass_send,
    pass_recv,
    own_sem,
):
    f = lax.axis_index("frames")
    h = lax.axis_index("heads")
    steps = frames // lanes
    hi = f // lanes
    lo = f % lanes
    piece = k_ref.shape[0]
    width = kv.shape[3]
    tokens = kv.shape[2]
    rows = q_ref.shape[0]
    q_local = q_ref.shape[1] // HEAD_DIM
    per_kv = q_local // (width // HEAD_DIM)
    mate = f + 1 - 2 * lo if lanes == 2 else f
    factor = HEAD_DIM**-0.5 * math.log2(math.e)

    barrier = pltpu.get_barrier_semaphore()

    def greet(d, carry):
        def one(r, inner):
            pl.semaphore_signal(
                barrier,
                inc=1,
                device_id=((hi - d) * lanes + lo, (h + r) % heads),
                device_id_type=MESH,
            )
            return inner

        return lax.fori_loop(jnp.where(d == 0, 1, 0), heads, one, carry)

    if lanes == 2:
        pl.semaphore_signal(barrier, inc=1, device_id=(mate, h), device_id_type=MESH)
    lax.fori_loop(0, hi + 1, greet, 0)
    pl.semaphore_wait(barrier, (steps - hi) * heads - 1 + (lanes - 1))

    def piece_copy(which, source, to_hi, to_h):
        target = to_hi * lanes + lo
        columns = pl.ds(pl.multiple_of(to_h * width, width), width)
        return pltpu.make_async_remote_copy(
            src_ref=source.at[:, columns],
            dst_ref=kv.at[f, which, pl.ds(pl.multiple_of(h * piece, piece), piece), :],
            send_sem=send_sem.at[to_hi - hi],
            recv_sem=recv_sem.at[hi],
            device_id=(target, to_h),
            device_id_type=MESH,
        )

    def send(i, carry):
        to_hi = steps - 1 - i
        start = jnp.where(to_hi == hi, 1, 0)

        def one(r, inner):
            to_h = (h + r) % heads
            piece_copy(0, k_ref, to_hi, to_h).start()
            piece_copy(1, v_ref, to_hi, to_h).start()
            return inner

        return lax.fori_loop(start, heads, one, carry)

    lax.fori_loop(0, steps - hi, send, 0)

    mine = pl.ds(pl.multiple_of(h * width, width), width)
    place = pl.ds(pl.multiple_of(h * piece, piece), piece)
    own = [
        pltpu.make_async_copy(source.at[:, mine], kv.at[f, which, place, :], own_sem.at[which])
        for which, source in ((0, k_ref), (1, v_ref))
    ]
    for copy in own:
        copy.start()

    for g in range(q_local):
        cols = slice(g * HEAD_DIM, (g + 1) * HEAD_DIM)
        qt[:, g * rows : (g + 1) * rows] = q_ref[:, cols].T
    top[...] = jnp.full_like(top, masked_score)
    total[...] = jnp.zeros_like(total)
    acc[...] = jnp.zeros_like(acc)
    for copy in own:
        copy.wait()

    def attend(group):
        limit = jnp.where(mask_ref[f, group] > 0, len_ref[group], 0)
        live = lax.broadcasted_iota(jnp.int32, (tokens, rows), 0) < limit
        for c in range(width // HEAD_DIM):
            cols = slice(c * HEAD_DIM, (c + 1) * HEAD_DIM)
            kb = kv[group, 0, :, cols]
            vt = kv[group, 1, :, cols].T
            for g in range(c * per_kv, (c + 1) * per_kv):
                at = slice(g * rows, (g + 1) * rows)
                s = jnp.dot(kb, qt[:, at], preferred_element_type=jnp.float32)
                s = jnp.where(live, s, masked_score)
                old = top[:, at]
                new = jnp.maximum(old, jnp.max(s, axis=0, keepdims=True))
                p = jnp.exp2((s - new) * factor)
                scale = jnp.exp2((old - new) * factor)
                top[:, at] = new
                total[:, at] = total[:, at] * scale + jnp.sum(p, axis=0, keepdims=True)
                acc[:, at] = acc[:, at] * scale + jnp.dot(
                    vt, p.astype(jnp.bfloat16), preferred_element_type=jnp.float32
                )

    def landed(group, sem):
        pltpu.make_async_copy(kv.at[group], kv.at[group], sem).wait()

    def pass_copy(group, slot):
        return pltpu.make_async_remote_copy(
            src_ref=kv.at[group],
            dst_ref=kv.at[group],
            send_sem=pass_send.at[slot],
            recv_sem=pass_recv.at[slot],
            device_id=(mate, h),
            device_id_type=MESH,
        )

    rest = kv.at[f, :, pl.ds(0, (heads - 1) * piece), :]
    pltpu.make_async_copy(rest, rest, recv_sem.at[hi]).wait()
    if lanes == 2:

        @pl.when(lo == 0)
        def _():
            pass_copy(f, hi).start()

    attend(f)

    def step(d, carry):
        from_hi = hi - d
        group = from_hi * lanes + lo
        landed(group, recv_sem.at[from_hi])
        if lanes == 2:
            pass_copy(group, from_hi).start()
        attend(group)
        if lanes == 2:
            other = from_hi * lanes + 1 - lo
            landed(other, pass_recv.at[from_hi])
            attend(other)
        return carry

    if lanes == 2:

        @pl.when(lo == 1)
        def _():
            landed(mate, pass_recv.at[hi])
            attend(mate)

    lax.fori_loop(1, hi + 1, step, 0)

    for g in range(q_local):
        at = slice(g * rows, (g + 1) * rows)
        done = (acc[:, at] / total[:, at]).T
        out_ref[:, g * HEAD_DIM : (g + 1) * HEAD_DIM] = done.astype(out_ref.dtype)

    pltpu.make_async_copy(rest, rest, send_sem.at[0]).wait()

    def drain(d, carry):
        pltpu.make_async_copy(kv.at[f], kv.at[f], send_sem.at[d]).wait()
        return carry

    lax.fori_loop(1, steps - hi, drain, 0)
    if lanes == 2:

        @pl.when(lo == 0)
        def _():
            pass_copy(f, hi).wait_send()

        def drain_pass(d, carry):
            pass_copy((hi - d) * lanes + lo, hi - d).wait_send()
            return carry

        lax.fori_loop(1, hi + 1, drain_pass, 0)


def solution(mesh):
    frames, heads = mesh.shape["frames"], mesh.shape["heads"]
    lanes = 2 if frames % 2 == 0 else 1

    def local(queries, keys, values, block_mask, lengths):
        rows, q_columns = queries.shape
        tokens = keys.shape[0] * heads
        width = keys.shape[1] // heads
        q_local = q_columns // HEAD_DIM
        steps = frames // lanes
        vmem = pl.BlockSpec(memory_space=pltpu.VMEM)
        smem = pl.BlockSpec(memory_space=pltpu.SMEM)
        return pl.pallas_call(
            functools.partial(kernel, frames, heads, lanes),
            out_shape=jax.ShapeDtypeStruct(queries.shape, queries.dtype),
            in_specs=[smem, smem, vmem, vmem, vmem],
            out_specs=vmem,
            scratch_shapes=[
                pltpu.VMEM((frames, 2, tokens, width), jnp.bfloat16),
                pltpu.VMEM((HEAD_DIM, q_local * rows), jnp.bfloat16),
                pltpu.VMEM((1, q_local * rows), jnp.float32),
                pltpu.VMEM((1, q_local * rows), jnp.float32),
                pltpu.VMEM((HEAD_DIM, q_local * rows), jnp.float32),
                pltpu.SemaphoreType.DMA((steps,)),
                pltpu.SemaphoreType.DMA((steps,)),
                pltpu.SemaphoreType.DMA((steps,)),
                pltpu.SemaphoreType.DMA((steps,)),
                pltpu.SemaphoreType.DMA((2,)),
            ],
            compiler_params=pltpu.CompilerParams(collective_id=0, has_side_effects=True),
        )(block_mask, lengths, queries, keys, values)

    return jax.shard_map(
        local,
        mesh=mesh,
        in_specs=(
            P("frames", "heads"),
            P(("frames", "heads"), None),
            P(("frames", "heads"), None),
            P(),
            P(),
        ),
        out_specs=P("frames", "heads"),
        check_vma=False,
    )
```

time: 84.8 us -> 23.7 us (0.28)
  the two profiles are of different devices: /device:TPU:30 before, /device:TPU:24 now
where the time goes in v1:
time: 23.7 us; the launch traced here: 23.6 us
  Pallas kernels  21.9 us (92%)
  local copies, waits for them, and re-layouts  1.67 us (7%)
    pallas_call x1, Pallas kernels, local(): pl.pallas_call(functools.partial(kernel, frames, heads, lanes), out_shape...  21.9 us
    unnamed x1, local copies, waits for them, and re-layouts  1.67 us

profile of v1, /device:TPU:24, one launch (start us, length us, event | category | flops | bytes accessed | tf_op | source)
XLA Modules:
  0.0 23.6 jit_solution(11399987142868235686)
XLA Ops:
  0.0 21.9 %shard_map.55 = bf16[128,1024]{1,0:T(8,128)(2,1)} custom-call(s32[8,8]{1,0:T(8,128)} %mask_ref.1, s32[8]{0:T(128)} %len_ref.1, bf16[128,1024]{1,0:T(8,128)(2,1)} %q_ref.1, bf16[32,512]{1,0:T(8,128)(2,1)} %k_ref.1, bf16[32,512]{1,0:T(8,128)(2,1)} %v_ref.1), custom_call_target="tpu_custom_call" | custom-call | tf_op jit(solution)/shard_map/pallas_call | solution.py:217
  21.9 1.7 %copy.7 = bf16[128,1024]{1,0:T(8,128)(2,1)} copy(bf16[128,1024]{1,0:T(8,128)(2,1)} %shard_map.55) | data formatting | bytes 524288

commit v2 on v1

v2 whole, which is shorter than its diff:
```python
import functools
import math

import jax
import jax.numpy as jnp
from jax import lax
from jax.experimental import pallas as pl
from jax.experimental.pallas import tpu as pltpu
from jax.sharding import PartitionSpec as P

HEAD_DIM = 128
MESH = pl.DeviceIdType.MESH
masked_score = -1e30


def kernel(
    frames,
    heads,
    lanes,
    mask_ref,
    len_ref,
    q_ref,
    k_ref,
    v_ref,
    out_ref,
    kv,
    q,
    qt,
    top,
    total,
    acc,
    mate_send,
    mate_recv,
    up_send,
    up_recv,
    side_send,
    side_recv,
    own_sem,
):
    f = lax.axis_index("frames")
    h = lax.axis_index("heads")
    steps = frames // lanes
    hi = f // lanes
    lo = f % lanes
    piece = k_ref.shape[0]
    width = kv.shape[3]
    tokens = kv.shape[2]
    rows = q_ref.shape[0]
    q_local = q_ref.shape[1] // HEAD_DIM
    per_kv = q_local // (width // HEAD_DIM)
    factor = HEAD_DIM**-0.5 * math.log2(math.e)
    partner = f + 1 - 2 * lo if lanes == 2 else f
    not_last = hi < steps - 1
    sends_side = (lo == 0) | (hi > 0)
    takes_side = (lo == 1) | (hi > 0)

    pair = 2 if heads % 2 == 0 else 1
    mates = [
        ((h // pair + j) % (heads // pair)) * pair + (h % pair + c) % pair
        for j in range(heads // pair)
        for c in range(pair)
    ][1:]

    barrier = pltpu.get_barrier_semaphore()

    def greet(device):
        pl.semaphore_signal(barrier, inc=1, device_id=device, device_id_type=MESH)

    @pl.when(hi > 0)
    def _():
        greet((f - lanes, h))

    for mate in mates:
        greet((f, mate))
    expected = heads - 1 + jnp.where(not_last, 1, 0)
    if lanes == 2:

        @pl.when(takes_side)
        def _():
            greet((partner, h))

        expected += jnp.where(sends_side, 1, 0)

    load_q = pltpu.make_async_copy(q_ref, q, own_sem.at[2])
    load_q.start()

    def rows_of(head):
        return pl.ds(pl.multiple_of(head * piece, piece), piece)

    mine = pl.ds(pl.multiple_of(h * width, width), width)
    sources = ((0, k_ref), (1, v_ref))
    own = [
        pltpu.make_async_copy(source.at[:, mine], kv.at[f, which, rows_of(h), :], own_sem.at[which])
        for which, source in sources
    ]
    for copy in own:
        copy.start()

    pl.semaphore_wait(barrier, expected)

    def remote(source, target, send, recv, device):
        return pltpu.make_async_remote_copy(
            src_ref=source,
            dst_ref=target,
            send_sem=send,
            recv_sem=recv,
            device_id=device,
            device_id_type=MESH,
        )

    for mate in mates[::-1]:
        columns = pl.ds(pl.multiple_of(mate * width, width), width)
        for which, source in sources:
            remote(
                source.at[:, columns],
                kv.at[f, which, rows_of(h), :],
                mate_send.at[0],
                mate_recv.at[h],
                (f, mate),
            ).start()

    def up(source, target, group_hi, head):
        remote(
            source, target, up_send.at[group_hi], up_recv.at[group_hi, head], (f + lanes, h)
        ).start()

    def side(source, target, group_hi):
        remote(
            source, target, side_send.at[group_hi], side_recv.at[group_hi], (partner, h)
        ).start()

    @pl.when(not_last)
    def _():
        for which, source in sources:
            up(source.at[:, mine], kv.at[f, which, rows_of(h), :], hi, h)

    if lanes == 2:

        @pl.when(lo == 0)
        def _():
            for which, source in sources:
                side(source.at[:, mine], kv.at[f, which, rows_of(h), :], hi)

    def landed(part, sem):
        pltpu.make_async_copy(part, part, sem).wait()

    def relay(group, group_hi, head, across):
        part = kv.at[group, :, rows_of(head), :]

        @pl.when(not_last)
        def _():
            up(part, part, group_hi, head)

        if lanes == 2:

            @pl.when(across)
            def _():
                side(part, part, group_hi)

    load_q.wait()
    for g in range(q_local):
        cols = slice(g * HEAD_DIM, (g + 1) * HEAD_DIM)
        qt[:, g * rows : (g + 1) * rows] = q[:, cols].T
    top[...] = jnp.full_like(top, masked_score)
    total[...] = jnp.zeros_like(total)
    acc[...] = jnp.zeros_like(acc)

    def attend(group):
        limit = jnp.where(mask_ref[f, group] > 0, len_ref[group], 0)
        live = lax.broadcasted_iota(jnp.int32, (tokens, rows), 0) < limit
        for c in range(width // HEAD_DIM):
            cols = slice(c * HEAD_DIM, (c + 1) * HEAD_DIM)
            kb = kv[group, 0, :, cols]
            vt = kv[group, 1, :, cols].T
            for g in range(c * per_kv, (c + 1) * per_kv):
                at = slice(g * rows, (g + 1) * rows)
                s = jnp.dot(kb, qt[:, at], preferred_element_type=jnp.float32)
                s = jnp.where(live, s, masked_score)
                old = top[:, at]
                new = jnp.maximum(old, jnp.max(s, axis=0, keepdims=True))
                p = jnp.exp2((s - new) * factor)
                scale = jnp.exp2((old - new) * factor)
                top[:, at] = new
                total[:, at] = total[:, at] * scale + jnp.sum(p, axis=0, keepdims=True)
                acc[:, at] = acc[:, at] * scale + jnp.dot(
                    vt, p.astype(jnp.bfloat16), preferred_element_type=jnp.float32
                )

    for mate in mates:
        landed(kv.at[f, :, rows_of(mate), :], mate_recv.at[mate])
        relay(f, hi, mate, lo == 0)
    for copy in own:
        copy.wait()
    attend(f)

    def attend_side(group_hi):
        group = group_hi * lanes + 1 - lo
        landed(kv.at[group], side_recv.at[group_hi])
        attend(group)

    def step(d, carry):
        group_hi = hi - d
        group = group_hi * lanes + lo
        for head in [h] + mates:
            landed(kv.at[group, :, rows_of(head), :], up_recv.at[group_hi, head])
            relay(group, group_hi, head, hi > 0)
        if lanes == 2:

            @pl.when((d > 1) | (lo == 1))
            def _():
                attend_side(group_hi + 1)

        attend(group)
        return carry

    lax.fori_loop(1, hi + 1, step, 0)
    if lanes == 2:

        @pl.when(takes_side)
        def _():
            attend_side(0)

    for g in range(q_local):
        at = slice(g * rows, (g + 1) * rows)
        done = (acc[:, at] / total[:, at]).T
        out_ref[:, g * HEAD_DIM : (g + 1) * HEAD_DIM] = done.astype(out_ref.dtype)

    rest = kv.at[f, :, pl.ds(0, (heads - 1) * piece), :]
    landed(rest, mate_send.at[0])

    @pl.when(not_last)
    def _():
        def drain(d, carry):
            landed(kv.at[f], up_send.at[hi - d])
            return carry

        lax.fori_loop(0, hi + 1, drain, 0)

    if lanes == 2:

        def drain_side(d, carry):
            landed(kv.at[f], side_send.at[hi - d])
            return carry

        lax.fori_loop(lo, hi + 1, drain_side, 0)


def solution(mesh):
    frames, heads = mesh.shape["frames"], mesh.shape["heads"]
    lanes = 2 if frames % 2 == 0 else 1

    def local(queries, keys, values, block_mask, lengths):
        rows, q_columns = queries.shape
        tokens = keys.shape[0] * heads
        width = keys.shape[1] // heads
        q_local = q_columns // HEAD_DIM
        steps = frames // lanes
        vmem = pl.BlockSpec(memory_space=pltpu.VMEM)
        hbm = pl.BlockSpec(memory_space=pl.ANY)
        smem = pl.BlockSpec(memory_space=pltpu.SMEM)
        return pl.pallas_call(
            functools.partial(kernel, frames, heads, lanes),
            out_shape=jax.ShapeDtypeStruct(queries.shape, queries.dtype),
            in_specs=[smem, smem, hbm, hbm, hbm],
            out_specs=vmem,
            scratch_shapes=[
                pltpu.VMEM((frames, 2, tokens, width), jnp.bfloat16),
                pltpu.VMEM(queries.shape, queries.dtype),
                pltpu.VMEM((HEAD_DIM, q_local * rows), jnp.bfloat16),
                pltpu.VMEM((1, q_local * rows), jnp.float32),
                pltpu.VMEM((1, q_local * rows), jnp.float32),
                pltpu.VMEM((HEAD_DIM, q_local * rows), jnp.float32),
                pltpu.SemaphoreType.DMA((1,)),
                pltpu.SemaphoreType.DMA((heads,)),
                pltpu.SemaphoreType.DMA((steps,)),
                pltpu.SemaphoreType.DMA((steps, heads)),
                pltpu.SemaphoreType.DMA((steps,)),
                pltpu.SemaphoreType.DMA((steps,)),
                pltpu.SemaphoreType.DMA((3,)),
            ],
            compiler_params=pltpu.CompilerParams(collective_id=0, has_side_effects=True),
        )(block_mask, lengths, queries, keys, values)

    return jax.shard_map(
        local,
        mesh=mesh,
        in_specs=(
            P("frames", "heads"),
            P(("frames", "heads"), None),
            P(("frames", "heads"), None),
            P(),
            P(),
        ),
        out_specs=P("frames", "heads"),
        check_vma=False,
    )
```

time: 23.7 us -> 19.4 us (0.82)
  Pallas kernels: 21.9 us -> 17.5 us
    pallas_call x1, Pallas kernels: 21.9 us -> 17.5 us  [local(): pl.pallas_call(functools.partial(kernel, frames, heads, lanes), out_shape...]
where the time goes in v2:
time: 19.4 us; the launch traced here: 19.2 us
  Pallas kernels  17.5 us (90%)
  local copies, waits for them, and re-layouts  1.67 us (9%)
    pallas_call x1, Pallas kernels, local(): pl.pallas_call(functools.partial(kernel, frames, heads, lanes), out_shape...  17.5 us
    unnamed x1, local copies, waits for them, and re-layouts  1.67 us

profile of v2, /device:TPU:24, one launch (start us, length us, event | category | flops | bytes accessed | tf_op | source)
XLA Modules:
  0.0 19.2 jit_solution(5702405409810000235)
XLA Ops:
  0.0 17.5 %shard_map.55 = bf16[128,1024]{1,0:T(8,128)(2,1)} custom-call(s32[8,8]{1,0:T(8,128)} %mask_ref.1, s32[8]{0:T(128)} %len_ref.1, bf16[128,1024]{1,0:T(8,128)(2,1)} %q_ref.1, bf16[32,512]{1,0:T(8,128)(2,1)} %k_ref.1, bf16[32,512]{1,0:T(8,128)(2,1)} %v_ref.1), custom_call_target="tpu_custom_call" | custom-call | tf_op jit(solution)/shard_map/pallas_call | solution.py:261
  17.5 1.7 %copy.7 = bf16[128,1024]{1,0:T(8,128)(2,1)} copy(bf16[128,1024]{1,0:T(8,128)(2,1)} %shard_map.55) | data formatting | bytes 524288

commit v3 on v2

--- a/solution.py
+++ b/solution.py
@@ -50,9 +50,6 @@
     per_kv = q_local // (width // HEAD_DIM)
     factor = HEAD_DIM**-0.5 * math.log2(math.e)
     partner = f + 1 - 2 * lo if lanes == 2 else f
-    not_last = hi < steps - 1
-    sends_side = (lo == 0) | (hi > 0)
-    takes_side = (lo == 1) | (hi > 0)
 
     pair = 2 if heads % 2 == 0 else 1
     mates = [
@@ -66,20 +63,17 @@
     def greet(device):
         pl.semaphore_signal(barrier, inc=1, device_id=device, device_id_type=MESH)
 
-    @pl.when(hi > 0)
-    def _():
-        greet((f - lanes, h))
-
-    for mate in mates:
+    def greet_down(from_hi, carry):
+        greet((from_hi * lanes + lo, h))
+        return carry
+
+    lax.fori_loop(0, hi, greet_down, 0)
+    for mate in mates[::-1]:
         greet((f, mate))
-    expected = heads - 1 + jnp.where(not_last, 1, 0)
-    if lanes == 2:
-
-        @pl.when(takes_side)
-        def _():
-            greet((partner, h))
-
-        expected += jnp.where(sends_side, 1, 0)
+    expected = heads - 1 + steps - 1 - hi
+    if lanes == 2:
+        greet((partner, h))
+        expected += 1
 
     load_q = pltpu.make_async_copy(q_ref, q, own_sem.at[2])
     load_q.start()
@@ -119,9 +113,13 @@
                 (f, mate),
             ).start()
 
-    def up(source, target, group_hi, head):
+    def up(source, target, to_hi, head):
         remote(
-            source, target, up_send.at[group_hi], up_recv.at[group_hi, head], (f + lanes, h)
+            source,
+            target,
+            up_send.at[to_hi],
+            up_recv.at[hi, head],
+            (to_hi * lanes + lo, h),
         ).start()
 
     def side(source, target, group_hi):
@@ -129,11 +127,6 @@
             source, target, side_send.at[group_hi], side_recv.at[group_hi], (partner, h)
         ).start()
 
-    @pl.when(not_last)
-    def _():
-        for which, source in sources:
-            up(source.at[:, mine], kv.at[f, which, rows_of(h), :], hi, h)
-
     if lanes == 2:
 
         @pl.when(lo == 0)
@@ -143,27 +136,6 @@
 
     def landed(part, sem):
         pltpu.make_async_copy(part, part, sem).wait()
-
-    def relay(group, group_hi, head, across):
-        part = kv.at[group, :, rows_of(head), :]
-
-        @pl.when(not_last)
-        def _():
-            up(part, part, group_hi, head)
-
-        if lanes == 2:
-
-            @pl.when(across)
-            def _():
-                side(part, part, group_hi)
-
-    load_q.wait()
-    for g in range(q_local):
-        cols = slice(g * HEAD_DIM, (g + 1) * HEAD_DIM)
-        qt[:, g * rows : (g + 1) * rows] = q[:, cols].T
-    top[...] = jnp.full_like(top, masked_score)
-    total[...] = jnp.zeros_like(total)
-    acc[...] = jnp.zeros_like(acc)
 
     def attend(group):
         limit = jnp.where(mask_ref[f, group] > 0, len_ref[group], 0)
@@ -186,39 +158,66 @@
                     vt, p.astype(jnp.bfloat16), preferred_element_type=jnp.float32
                 )
 
+    far = steps - 1
+
+    def up_all(head, parts):
+        def one(d, carry):
+            for source, target in parts:
+                up(source, target, far - d, head)
+            return carry
+
+        lax.fori_loop(0, far - hi, one, 0)
+
+    up_all(
+        h, [(source.at[:, mine], kv.at[f, which, rows_of(h), :]) for which, source in sources]
+    )
+    load_q.wait()
+    for g in range(q_local):
+        cols = slice(g * HEAD_DIM, (g + 1) * HEAD_DIM)
+        qt[:, g * rows : (g + 1) * rows] = q[:, cols].T
+    top[...] = jnp.full_like(top, masked_score)
+    total[...] = jnp.zeros_like(total)
+    acc[...] = jnp.zeros_like(acc)
     for mate in mates:
-        landed(kv.at[f, :, rows_of(mate), :], mate_recv.at[mate])
-        relay(f, hi, mate, lo == 0)
+        part = kv.at[f, :, rows_of(mate), :]
+        landed(part, mate_recv.at[mate])
+        up_all(mate, [(part, part)])
+        if lanes == 2:
+
+            @pl.when(lo == 0)
+            def _():
+                side(part, part, hi)
+
     for copy in own:
         copy.wait()
-    attend(f)
-
-    def attend_side(group_hi):
-        group = group_hi * lanes + 1 - lo
-        landed(kv.at[group], side_recv.at[group_hi])
-        attend(group)
 
     def step(d, carry):
         group_hi = hi - d
         group = group_hi * lanes + lo
-        for head in [h] + mates:
-            landed(kv.at[group, :, rows_of(head), :], up_recv.at[group_hi, head])
-            relay(group, group_hi, head, hi > 0)
-        if lanes == 2:
-
-            @pl.when((d > 1) | (lo == 1))
-            def _():
-                attend_side(group_hi + 1)
-
-        attend(group)
+
+        @pl.when(d <= hi)
+        def _():
+            for head in [h] + mates:
+                part = kv.at[group, :, rows_of(head), :]
+                landed(part, up_recv.at[group_hi, head])
+                if lanes == 2:
+                    side(part, part, group_hi)
+
+        attend(group + lanes)
         return carry
 
-    lax.fori_loop(1, hi + 1, step, 0)
-    if lanes == 2:
-
-        @pl.when(takes_side)
-        def _():
-            attend_side(0)
+    lax.fori_loop(1, hi + 2, step, 0)
+
+    if lanes == 2:
+
+        def step_side(d, carry):
+            group_hi = hi - d
+            group = group_hi * lanes + 1 - lo
+            landed(kv.at[group], side_recv.at[group_hi])
+            attend(group)
+            return carry
+
+        lax.fori_loop(1 - lo, hi + 1, step_side, 0)
 
     for g in range(q_local):
         at = slice(g * rows, (g + 1) * rows)
@@ -228,14 +227,11 @@
     rest = kv.at[f, :, pl.ds(0, (heads - 1) * piece), :]
     landed(rest, mate_send.at[0])
 
-    @pl.when(not_last)
-    def _():
-        def drain(d, carry):
-            landed(kv.at[f], up_send.at[hi - d])
-            return carry
-
-        lax.fori_loop(0, hi + 1, drain, 0)
-
+    def drain(to_hi, carry):
+        landed(kv.at[f], up_send.at[to_hi])
+        return carry
+
+    lax.fori_loop(hi + 1, steps, drain, 0)
     if lanes == 2:
 
         def drain_side(d, carry):

time: 19.4 us -> 18.3 us (0.943)
  the two profiles are of different devices: /device:TPU:24 before, /device:TPU:20 now
where the time goes in v3:
time: 18.3 us; the launch traced here: 18.1 us
  Pallas kernels  16.4 us (90%)
  local copies, waits for them, and re-layouts  1.67 us (9%)
    pallas_call x1, Pallas kernels, local(): pl.pallas_call(functools.partial(kernel, frames, heads, lanes), out_shape...  16.4 us
    unnamed x1, local copies, waits for them, and re-layouts  1.67 us

profile of v3, /device:TPU:20, one launch (start us, length us, event | category | flops | bytes accessed | tf_op | source)
XLA Modules:
  0.0 18.1 jit_solution(16766000840001454513)
XLA Ops:
  0.0 16.4 %shard_map.55 = bf16[128,1024]{1,0:T(8,128)(2,1)} custom-call(s32[8,8]{1,0:T(8,128)} %mask_ref.1, s32[8]{0:T(128)} %len_ref.1, bf16[128,1024]{1,0:T(8,128)(2,1)} %q_ref.1, bf16[32,512]{1,0:T(8,128)(2,1)} %k_ref.1, bf16[32,512]{1,0:T(8,128)(2,1)} %v_ref.1), custom_call_target="tpu_custom_call" | custom-call | tf_op jit(solution)/shard_map/pallas_call | solution.py:257
  16.4 1.7 %copy.7 = bf16[128,1024]{1,0:T(8,128)(2,1)} copy(bf16[128,1024]{1,0:T(8,128)(2,1)} %shard_map.55) | data formatting | bytes 524288

commit v4 on v3

--- a/solution.py
+++ b/solution.py
@@ -17,8 +17,8 @@
     frames,
     heads,
     lanes,
-    mask_ref,
-    len_ref,
+    mask_in,
+    len_in,
     q_ref,
     k_ref,
     v_ref,
@@ -36,6 +36,8 @@
     side_send,
     side_recv,
     own_sem,
+    mask_ref,
+    len_ref,
 ):
     f = lax.axis_index("frames")
     h = lax.axis_index("heads")
@@ -77,6 +79,12 @@
 
     load_q = pltpu.make_async_copy(q_ref, q, own_sem.at[2])
     load_q.start()
+    tables = [
+        pltpu.make_async_copy(mask_in, mask_ref, own_sem.at[3]),
+        pltpu.make_async_copy(len_in, len_ref, own_sem.at[4]),
+    ]
+    for copy in tables:
+        copy.start()
 
     def rows_of(head):
         return pl.ds(pl.multiple_of(head * piece, piece), piece)
@@ -172,6 +180,8 @@
         h, [(source.at[:, mine], kv.at[f, which, rows_of(h), :]) for which, source in sources]
     )
     load_q.wait()
+    for copy in tables:
+        copy.wait()
     for g in range(q_local):
         cols = slice(g * HEAD_DIM, (g + 1) * HEAD_DIM)
         qt[:, g * rows : (g + 1) * rows] = q[:, cols].T
@@ -252,12 +262,15 @@
         q_local = q_columns // HEAD_DIM
         steps = frames // lanes
         vmem = pl.BlockSpec(memory_space=pltpu.VMEM)
-        hbm = pl.BlockSpec(memory_space=pl.ANY)
-        smem = pl.BlockSpec(memory_space=pltpu.SMEM)
+        hbm = pl.BlockSpec(memory_space=pltpu.HBM)
+        pinned = [
+            pltpu.with_memory_space_constraint(array, pltpu.HBM)
+            for array in (block_mask, lengths, queries, keys, values)
+        ]
         return pl.pallas_call(
             functools.partial(kernel, frames, heads, lanes),
             out_shape=jax.ShapeDtypeStruct(queries.shape, queries.dtype),
-            in_specs=[smem, smem, hbm, hbm, hbm],
+            in_specs=[hbm] * 5,
             out_specs=vmem,
             scratch_shapes=[
                 pltpu.VMEM((frames, 2, tokens, width), jnp.bfloat16),
@@ -272,10 +285,16 @@
                 pltpu.SemaphoreType.DMA((steps, heads)),
                 pltpu.SemaphoreType.DMA((steps,)),
                 pltpu.SemaphoreType.DMA((steps,)),
-                pltpu.SemaphoreType.DMA((3,)),
+                pltpu.SemaphoreType.DMA((5,)),
+                pltpu.SMEM(block_mask.shape, jnp.int32),
+                pltpu.SMEM(lengths.shape, jnp.int32),
             ],
-            compiler_params=pltpu.CompilerParams(collective_id=0, has_side_effects=True),
-        )(block_mask, lengths, queries, keys, values)
+            compiler_params=pltpu.CompilerParams(
+                collective_id=0,
+                has_side_effects=True,
+                vmem_limit_bytes=frames * 4 * tokens * width + (8 << 20),
+            ),
+        )(*pinned)
 
     return jax.shard_map(
         local,

time: 18.3 us -> 15.8 us (0.86)
  Pallas kernels: 16.4 us -> 15 us
  local copies, waits for them, and re-layouts: 1.67 us -> 0.71 us
    pallas_call x1, Pallas kernels: 16.4 us -> 15 us  [local(): pl.pallas_call(functools.partial(kernel, frames, heads, lanes), out_shape...]
    unnamed x1, local copies, waits for them, and re-layouts: 1.67 us -> 0.71 us
where the time goes in v4:
time: 15.8 us; the launch traced here: 15.7 us
  Pallas kernels  15 us (95%)
  local copies, waits for them, and re-layouts  0.71 us (4%)
    pallas_call x1, Pallas kernels, local(): pl.pallas_call(functools.partial(kernel, frames, heads, lanes), out_shape...  15 us
    unnamed x1, local copies, waits for them, and re-layouts  0.71 us

profile of v4, /device:TPU:20, one launch (start us, length us, event | category | flops | bytes accessed | tf_op | source)
XLA Modules:
  0.0 15.7 jit_solution(14711860286390562757)
XLA Ops:
  0.0 15.0 %shard_map.55 = bf16[128,1024]{1,0:T(8,128)(2,1)S(1)} custom-call(s32[8,8]{1,0:T(8,128)} %mask_in.1, s32[8]{0:T(128)} %len_in.1, bf16[128,1024]{1,0:T(8,128)(2,1)} %q_ref.1, bf16[32,512]{1,0:T(8,128)(2,1)} %k_ref.1, bf16[32,512]{1,0:T(8,128)(2,1)} %v_ref.1), custom_call_target="tpu_custom_call" | custom-call | tf_op jit(solution)/shard_map/pallas_call | solution.py:270
  15.0 0.7 %copy.7 = bf16[128,1024]{1,0:T(8,128)(2,1)} copy(bf16[128,1024]{1,0:T(8,128)(2,1)S(1)} %shard_map.55) | data formatting | bytes 524288

commit v5 on v4

--- a/solution.py
+++ b/solution.py
@@ -126,7 +126,7 @@
             source,
             target,
             up_send.at[to_hi],
-            up_recv.at[hi, head],
+            up_recv.at[hi, head // pair],
             (to_hi * lanes + lo, h),
         ).start()
 
@@ -207,9 +207,11 @@
 
         @pl.when(d <= hi)
         def _():
-            for head in [h] + mates:
-                part = kv.at[group, :, rows_of(head), :]
-                landed(part, up_recv.at[group_hi, head])
+            for head in ([h] + mates)[::pair]:
+                both = head // pair
+                span = pl.ds(pl.multiple_of(both * pair * piece, pair * piece), pair * piece)
+                part = kv.at[group, :, span, :]
+                landed(part, up_recv.at[group_hi, both])
                 if lanes == 2:
                     side(part, part, group_hi)
 
@@ -282,7 +284,7 @@
                 pltpu.SemaphoreType.DMA((1,)),
                 pltpu.SemaphoreType.DMA((heads,)),
                 pltpu.SemaphoreType.DMA((steps,)),
-                pltpu.SemaphoreType.DMA((steps, heads)),
+                pltpu.SemaphoreType.DMA((steps, heads // (2 if heads % 2 == 0 else 1))),
                 pltpu.SemaphoreType.DMA((steps,)),
                 pltpu.SemaphoreType.DMA((steps,)),
                 pltpu.SemaphoreType.DMA((5,)),

time: 15.8 us -> 15.9 us (level)
  no operation moved by 1% of the time
where the time goes in v5:
time: 15.9 us; the launch traced here: 15.8 us
  Pallas kernels  15 us (94%)
  local copies, waits for them, and re-layouts  0.71 us (4%)
    pallas_call x1, Pallas kernels, local(): pl.pallas_call(functools.partial(kernel, frames, heads, lanes), out_shape...  15 us
    unnamed x1, local copies, waits for them, and re-layouts  0.71 us

profile of v5, /device:TPU:20, one launch (start us, length us, event | category | flops | bytes accessed | tf_op | source)
XLA Modules:
  0.0 15.8 jit_solution(2327397655660634213)
XLA Ops:
  0.0 15.0 %shard_map.55 = bf16[128,1024]{1,0:T(8,128)(2,1)S(1)} custom-call(s32[8,8]{1,0:T(8,128)} %mask_in.1, s32[8]{0:T(128)} %len_in.1, bf16[128,1024]{1,0:T(8,128)(2,1)} %q_ref.1, bf16[32,512]{1,0:T(8,128)(2,1)} %k_ref.1, bf16[32,512]{1,0:T(8,128)(2,1)} %v_ref.1), custom_call_target="tpu_custom_call" | custom-call | tf_op jit(solution)/shard_map/pallas_call | solution.py:272
  15.1 0.7 %copy.7 = bf16[128,1024]{1,0:T(8,128)(2,1)} copy(bf16[128,1024]{1,0:T(8,128)(2,1)S(1)} %shard_map.55) | data formatting | bytes 524288
